TPU v7x, 256 devices: a whole 4x4x8 slice. The times are simulated.
256 devices in a mesh: rep: 8 (over z_lo, y), inner: 32 (over z_hi, x, core).
Axes of the slice: x: 4, y: 4, z: 8 (z_hi: 4, z_lo: 2; z = z_hi * 2 + z_lo), core: 2. Of those that a mesh axis runs over, the one named last changes fastest.
Arguments:
- local_weights: float32 [8, 12, 1600, 1600], P('rep', None, 'inner'), may hold values from -6 to 6
- owner_global: float32 [32, 1600, 1600], P('inner', None, 'rep'), may hold values from -6 to 6
- owner_momentum: float32 [32, 1600, 1600], P('inner', None, 'rep'), may hold values from -6 to 6
- owner_list: int32 [12], replicated, may hold values from 0 to 31, as said below
- local_down: float32 [8, 6400, 1600], P('rep', 'inner'), may hold values from -6 to 6
- global_down: float32 [6400, 1600], P('inner', 'rep'), may hold values from -6 to 6
- down_basis: float32 [6400, 64], P('inner'), may hold values from -0.15625 to 0.15625
- coef_momentum: float32 [64, 1600], P(None, 'rep'), may hold values from -6 to 6
Outputs:
- new_weights: float32 [12, 1600, 1600], P(None, 'inner')
- momentum_out: float32 [32, 1600, 1600], P('inner', None, 'rep')
- new_down: float32 [6400, 1600], P('inner', 'rep')
- coef_new: float32 [64, 1600], P(None, 'rep')
Inputs may be any that keep to these rules, and one draw needn't show every extreme that they name: `owner_list`: the 12 entries are distinct inner indices; both ends of the range are owners.
All inputs are finite; a program needn't handle non-finite values.
Results may differ from a plain program's by a relative error of at most 0.00007.
Values sent between devices are 32-bit elements; how exact they have to be, the bound alone decides.
A program may use at most 128 MiB of HBM per device.

v0:
```python
import jax
import jax.numpy as jnp
from jax import lax
from jax.sharding import PartitionSpec as P

outer_momentum = 0.9
outer_rate = 0.7


def project_rows(basis, values):
    return lax.dot_general(
        basis,
        values,
        (((0,), (0,)), ((), ())),
        precision=lax.Precision.HIGHEST,
        preferred_element_type=jnp.float32,
    )


def on_device(
    local_weights,
    owner_global,
    owner_momentum,
    owner_list,
    local_down,
    global_down,
    down_basis,
    coef_momentum,
):
    groups = lax.axis_size("rep")
    owners = lax.axis_size("inner")
    inner_index = lax.axis_index("inner")
    width = global_down.shape[1]
    col_start = lax.axis_index("rep") * width
    block = local_weights[0]
    matrices = block.shape[0]
    slab = block.shape[1]
    order = jnp.arange(matrices, dtype=jnp.int32)
    match = (owner_list[None, :] == jnp.arange(owners, dtype=jnp.int32)[:, None]).astype(jnp.int32)
    owned = (jnp.sum(match, axis=1) > 0).astype(jnp.float32)
    picked = jnp.sum(match * order[None, :], axis=1)
    down_local = project_rows(down_basis, local_down[0])
    down_global = project_rows(down_basis, global_down)
    summed = lax.psum_scatter(block, "rep", scatter_dimension=2, tiled=True)
    placed = lax.dynamic_update_slice_in_dim(jnp.zeros_like(down_local), down_global, col_start, 1)
    total = lax.psum(placed - down_local / groups, ("rep", "inner"))
    coef_step = lax.dynamic_slice_in_dim(total, col_start, width, 1)
    average = summed / groups
    current = owner_global[0]
    moment = owner_momentum[0]
    outgoing = average[picked] * owned[:, None, None]
    arrived = lax.all_to_all(outgoing, "inner", split_axis=0, concat_axis=0, tiled=True).reshape(
        owners * slab, width
    )
    delta = current - arrived
    moment_new = outer_momentum * moment + delta
    theta = current - outer_rate * (delta + outer_momentum * moment_new)
    is_owner = jnp.sum((owner_list == inner_index).astype(jnp.float32))
    momentum_out = (moment_new * is_owner)[None]
    returned = lax.all_to_all(
        theta.reshape(owners, slab, width), "inner", split_axis=0, concat_axis=0, tiled=True
    )
    updated = returned[owner_list]
    new_weights = lax.all_gather(updated, "rep", axis=2, tiled=True)
    coef_new = outer_momentum * coef_momentum + coef_step
    change = jnp.dot(
        down_basis,
        coef_step + outer_momentum * coef_new,
        precision=lax.Precision.HIGHEST,
        preferred_element_type=jnp.float32,
    )
    new_down = global_down - outer_rate * change
    return (new_weights, momentum_out, new_down, coef_new)


def solution(mesh):
    in_specs = (
        P("rep", None, "inner", None),
        P("inner", None, "rep"),
        P("inner", None, "rep"),
        P(),
        P("rep", "inner", None),
        P("inner", "rep"),
        P("inner", None),
        P(None, "rep"),
    )
    out_specs = (P(None, "inner", None), P("inner", None, "rep"), P("inner", "rep"), P(None, "rep"))
    return jax.shard_map(
        on_device, mesh=mesh, in_specs=in_specs, out_specs=out_specs, check_vma=False
    )
```

profile of v0, /device:TPU:1, one launch (start us, length us, event | category | flops | bytes accessed | tf_op | source)
XLA Modules:
  0.0 587.9 jit_solution(15279377533316422879)
XLA Ops:
  8.0 0.0 copy-start
  8.0 0.0 all-reduce.6.cloned.1.call-start
  8.1 4.6 copy.44
  12.7 0.0 copy-start.7
  12.7 0.0 copy-start.6
  12.7 0.0 all-reduce.6.cloned.1.call-update
  12.7 0.6 copy-done.7
  13.4 0.6 dynamic-slice
  14.6 0.0 copy-done.6
  14.6 0.1 convert_reduce_fusion
  14.7 118.1 %all-reduce.6.cloned.1.call-done = f32[12,50,1600]{2,1,0:T(8,128)} async-done(((f32[12,50,1600]{2,1,0:T(8,128)}), f32[12,50,1600]{2,1,0:T(8,128)}) %all-reduce.6.cloned.1.call-update) | async-done | bytes 3840016
  132.8 1.5 dynamic-slice_multiply_fusion
  134.3 1.9 gather_fusion
  136.2 2.9 broadcast_multiply_fusion
  139.1 9.4 %all-to-all-start = ((f32[32,50,200]{2,1,0:T(8,128)}), f32[32,50,200]{2,1,0:T(8,128)S(1)}, u32[]{:S(2)}, u32[]{:S(2)}) async-start(f32[32,50,200]{2,1,0:T(8,128)} %broadcast_multiply_fusion), calls=%async_computation | async-start | bytes 3670016 | tf_op jit(solution)/shard_map/all_to_all | solution.py:52
  148.5 3.0 copy.32
  151.5 3.0 copy.33
  154.5 2.6 squeeze.10
  157.0 0.6 fusion.8
  157.6 27.2 %all-to-all-done = f32[32,50,200]{2,1,0:T(8,128)S(1)} async-done(((f32[32,50,200]{2,1,0:T(8,128)}), f32[32,50,200]{2,1,0:T(8,128)S(1)}, u32[]{:S(2)}, u32[]{:S(2)}) %all-to-all-start) | async-done | bytes 1280032 | tf_op jit(solution)/shard_map/all_to_all | solution.py:52
  184.9 1.4 reshape.35
  186.2 5.1 add_multiply_fusion
  191.3 2.6 mul.65
  193.9 3.8 multiply_subtract_fusion
  197.7 0.0 copy-start.2
  197.7 0.0 copy-start.3
  197.7 14.4 %all-to-all-start.1 = ((f32[32,50,200]{2,1,0:T(8,128)}), f32[32,50,200]{2,1,0:T(8,128)S(1)}, u32[]{:S(2)}, u32[]{:S(2)}) async-start(f32[32,50,200]{2,1,0:T(8,128)} %multiply_subtract_fusion), calls=%async_computation.1 | async-start | bytes 3670016 | tf_op jit(solution)/shard_map/all_to_all | solution.py:60
  212.2 0.0 all-reduce.4.cloned.1.call-start
  212.2 0.0 copy-done.2
  212.2 0.0 copy-done.3
  212.3 0.2 fusion.12
  212.5 0.8 broadcast_in_dim.5
  213.3 1.5 dynamic_update_slice.3
  214.8 0.0 copy-done
  214.8 2.7 fusion
  217.5 0.0 all-reduce.4.cloned.1.call-update
  217.5 0.0 all-gather.3.cloned.1.call-start
  217.6 30.9 %all-to-all-done.1 = f32[32,50,200]{2,1,0:T(8,128)S(1)} async-done(((f32[32,50,200]{2,1,0:T(8,128)}), f32[32,50,200]{2,1,0:T(8,128)S(1)}, u32[]{:S(2)}, u32[]{:S(2)}) %all-to-all-start.1) | async-done | bytes 1280032 | tf_op jit(solution)/shard_map/all_to_all | solution.py:60
  248.5 1.4 gather_fusion.1
  249.9 0.0 copy-start.5
  249.9 3.1 copy.34
  253.0 0.0 copy-start.1
  253.0 0.0 all-gather.3.cloned.1.call-update
  253.0 0.8 copy.36
  253.8 311.1 %all-reduce.4.cloned.1.call-done = f32[64,1600]{1,0:T(8,128)} async-done(((f32[64,1600]{1,0:T(8,128)}), f32[64,1600]{1,0:T(8,128)}) %all-reduce.4.cloned.1.call-update) | async-done | bytes 409616 | tf_op jit(solution)/shard_map/psum | solution.py:46
  564.9 0.0 copy-done.5
  564.9 1.0 multiply_add_fusion
  565.9 0.0 copy-start.4
  565.9 1.4 fusion.3
  567.4 0.8 copy.39
  568.2 0.0 copy-done.1
  568.2 1.6 copy.38
  569.7 0.0 copy-done.4
  569.8 0.0 all-gather.3.cloned.1.call-done
  569.8 10.7 %copy.37 = f32[12,50,1600]{2,1,0:T(8,128)} copy(f32[12,50,1600]{1,0,2:T(8,128)} %all-gather.3.cloned.1.call-done) | data formatting | bytes 7680000
  (5 shorter events, 0.0 us)
Async XLA Ops:
  8.0 206.8 %copy-start = (f32[1,200,1600]{2,1,0:T(8,128)S(1)}, f32[1,200,1600]{2,1,0:T(8,128)}, u32[]{:S(2)}) copy-start(f32[1,200,1600]{2,1,0:T(8,128)} %param.12) | copy-start | bytes 3840004
  8.0 124.8 %all-reduce.6.cloned.1.call-start = ((), (), s32[]{:S(2)}) async-start(), calls=%async_computation.4 | async-start | bytes 8945664
  12.7 0.7 copy-start.7
  12.7 1.9 copy-start.6
  139.1 45.7 %all-to-all-start = ((f32[32,50,200]{2,1,0:T(8,128)}), f32[32,50,200]{2,1,0:T(8,128)S(1)}, u32[]{:S(2)}, u32[]{:S(2)}) async-start(f32[32,50,200]{2,1,0:T(8,128)} %broadcast_multiply_fusion), calls=%async_computation | async-start | bytes 3670016 | tf_op jit(solution)/shard_map/all_to_all | solution.py:52
  197.7 14.5 %copy-start.2 = (f32[200,200]{1,0:T(8,128)S(1)}, f32[200,200]{1,0:T(8,128)}, u32[]{:S(2)}) copy-start(f32[200,200]{1,0:T(8,128)} %param.13) | copy-start | bytes 480004
  197.7 14.5 %copy-start.3 = (f32[200,64]{0,1:T(8,128)S(1)}, f32[200,64]{0,1:T(8,128)}, u32[]{:S(2)}) copy-start(f32[200,64]{0,1:T(8,128)} %param.14) | copy-start | bytes 153604
  197.7 50.7 %all-to-all-start.1 = ((f32[32,50,200]{2,1,0:T(8,128)}), f32[32,50,200]{2,1,0:T(8,128)S(1)}, u32[]{:S(2)}, u32[]{:S(2)}) async-start(f32[32,50,200]{2,1,0:T(8,128)} %multiply_subtract_fusion), calls=%async_computation.1 | async-start | bytes 3670016 | tf_op jit(solution)/shard_map/all_to_all | solution.py:60
  212.2 352.8 %all-reduce.4.cloned.1.call-start = ((), (), s32[]{:S(2)}) async-start(), calls=%async_computation.2 | async-start | bytes 851968 | tf_op jit(solution)/shard_map/psum | solution.py:46
  217.5 352.2 %all-gather.3.cloned.1.call-start = ((), (), s32[]{:S(2)}) async-start(), calls=%async_computation.3 | async-start | bytes 14745600 | tf_op jit(solution)/shard_map/all_gather | solution.py:64
  249.9 315.0 %copy-start.5 = (f32[64,200]{1,0:T(8,128)S(1)}, f32[64,200]{1,0:T(8,128)}, u32[]{:S(2)}) copy-start(f32[64,200]{1,0:T(8,128)} %param.15) | copy-start | bytes 153604
  253.0 315.2 %copy-start.1 = (f32[1,1600,200]{2,1,0:T(8,128)S(1)}, f32[1,1600,200]{2,1,0:T(8,128)}, u32[]{:S(2)}) copy-start(f32[1,1600,200]{2,1,0:T(8,128)} %get-tuple-element.22) | copy-start | bytes 3840004
  565.9 3.8 copy-start.4
Sparse Core Ops, SparseCore 0:
  12.9 119.9 all-reduce.5
  253.2 144.6 all-gather.2
Sparse Core Ops, SparseCore 1:
  219.1 345.8 all-reduce.3
where the time goes:
time: 589 us; the launch traced here: 588 us
  waiting for transfers between devices  487 us (83%)
  local copies, waits for them, and re-layouts  41 us (7%)
  starting transfers between devices  23.9 us (4%)
  between operations  16.3 us (3%)
  other arithmetic  15 us (3%)
    psum x1, waiting for transfers between devices, on_device(): total = lax.psum(placed - down_local / groups, ('rep', 'inner'))  311 us
    unnamed x4, waiting for transfers between devices  118 us
    all_to_all x1, waiting for transfers between devices, on_device(): lax.all_to_all(theta.reshape(owners, slab, width), 'inner', split_axis=0,...  30.9 us
    all_to_all x1, waiting for transfers between devices, on_device(): lax.all_to_all(outgoing, 'inner', split_axis=0, concat_axis=0, tiled=True)  27.2 us
    unnamed x24, local copies, waits for them, and re-layouts  25.8 us
    all_to_all x1, starting transfers between devices, on_device(): lax.all_to_all(theta.reshape(owners, slab, width), 'inner', split_axis=0,...  14.4 us
  transfers between devices with their start and end apart: 5, of which 4 were waited for; matrix products, arithmetic and copies ran while one was open for 4% of the time, Pallas kernels for 0%

commit v1 on v0

v1 whole, which is shorter than its diff:
```python
import jax
import jax.numpy as jnp
from jax import lax
from jax.experimental import pallas as pl
from jax.experimental.pallas import tpu as pltpu
from jax.sharding import PartitionSpec as P

MESH = pl.DeviceIdType.MESH
HIGHEST = lax.Precision.HIGHEST
F32 = jnp.float32

outer_momentum = 0.9
outer_rate = 0.7

D = 1600
MATS = 12
HALF = MATS // 2
GROUPS = 8
OWNERS = 32
WIDTH = D // GROUPS
SLAB = D // OWNERS
RANK = 64
FOLD = 5
SUB = WIDTH // FOLD
LANES = 256
Y, ZLO, ZHI, XC = 4, 2, 4, 8

AVERAGE_PART = outer_rate * (1.0 + outer_momentum)
CURRENT_PART = 1.0 - AVERAGE_PART
MOMENT_PART = -outer_rate * outer_momentum * outer_momentum


def fold_lanes(parts):
    pad = jnp.zeros(parts[0].shape[:-1] + (LANES - FOLD * SLAB,), F32)
    return jnp.concatenate(list(parts) + [pad], axis=-1)


def pack_kernel(w_ref, g_ref, m_ref, bt_ref, ld_ref, gd_ref, wp_ref, bp_ref, cp_ref):
    cols = w_ref[0].T.reshape(ZLO, Y, FOLD, SUB, SLAB)
    wp_ref[:, 0] = fold_lanes([cols[:, :, g] for g in range(FOLD)]).transpose(1, 0, 2, 3)

    @pl.when(pl.program_id(0) == 0)
    def _():
        b = (CURRENT_PART * g_ref[...] + MOMENT_PART * m_ref[...]).reshape(FOLD, SUB, D)
        for i in range(OWNERS):
            bp_ref[i] = fold_lanes([b[g][:, SLAB * i : SLAB * (i + 1)] for g in range(FOLD)])

    @pl.when(pl.program_id(0) == 1)
    def _():
        rep = lax.axis_index("rep")
        local = jnp.dot(bt_ref[...], ld_ref[...], precision=HIGHEST, preferred_element_type=F32)
        mine = jnp.dot(bt_ref[...], gd_ref[...], precision=HIGHEST, preferred_element_type=F32)
        pad = jnp.zeros((RANK, LANES - WIDTH), F32)
        for r in range(GROUPS):
            part = local[:, WIDTH * r : WIDTH * (r + 1)] * (-1.0 / GROUPS)
            part = part + jnp.where(rep == r, mine, 0.0)
            cp_ref[:, r % Y, r // Y] = jnp.concatenate([part, pad], axis=-1).reshape(
                XC, RANK // XC, LANES
            )


def comm_kernel(
    list_ref, wp, bp, cp, out, arec, coef,
    r1p, r1m, r2p, r2m, sp, sm, rz, ssum, avg, brec, asend,
    d1, d2, d3, d4, e2, f2, g2,
    s_one, s_two, s_rel, s_z, s_own, s_fwd, s_far, s_b, s_a, s_d1, s_d2, s_dz, s_d3, s_d4,
    q_one, q_two, q_z, q_out, q_b, q_a, q_d1, q_d2, q_dz, q_d3, q_d4,
):
    rep, inner = lax.axis_index("rep"), lax.axis_index("inner")
    y, zl = lax.rem(rep, Y), rep // Y
    xc, zh = lax.rem(inner, XC), inner // XC
    up, down, far = lax.rem(y + 1, Y), lax.rem(y + 3, Y), lax.rem(y + 2, Y)
    right, left, pair = (zl * Y + up, inner), (zl * Y + down, inner), ((1 - zl) * Y + y, inner)

    def copy(src, dst, send, recv, to):
        return pltpu.make_async_remote_copy(
            src_ref=src, dst_ref=dst, send_sem=send, recv_sem=recv, device_id=to, device_id_type=MESH
        )

    def arrived(dst, recv):
        copy(dst, dst, s_one.at[0], recv, right).wait_recv()

    def left_it(src, send):
        copy(src, src, send, q_one.at[0], right).wait_send()


    @pl.loop(0, HALF)
    def _(k):
        copy(wp.at[far, k], r1p.at[k], s_one.at[k], q_one.at[k], right).start()
        copy(wp.at[far, HALF + k], r1m.at[k], s_one.at[HALF + k], q_one.at[HALF + k], left).start()

    @pl.loop(1, XC)
    def _(k):
        q = lax.rem(xc + k, XC)
        copy(cp.at[q], d1.at[xc], s_d1.at[q], q_d1.at[xc], (rep, zh * XC + q)).start()

    @pl.loop(0, HALF)
    def _(k):
        copy(wp.at[up, HALF + k], r2p.at[HALF + k], s_two.at[k], q_two.at[k], right).start()
        copy(wp.at[down, k], r2m.at[k], s_two.at[HALF + k], q_two.at[HALF + k], left).start()

    @pl.loop(1, OWNERS)
    def _(k):
        i = lax.rem(inner + k, OWNERS)
        copy(bp.at[i], brec.at[inner], s_b.at[i], q_b.at[inner], (rep, i)).start()

    brec[inner] = bp[inner]

    @pl.loop(0, HALF)
    def _(k):
        arrived(r1p.at[k], q_one.at[k])
        sp[k] = r1p[k] + wp[up, k]
        copy(sp.at[k], r2p.at[k], s_rel.at[k], q_two.at[MATS + k], right).start()
        arrived(r1m.at[k], q_one.at[HALF + k])
        sm[k] = r1m[k] + wp[down, HALF + k]
        copy(sm.at[k], r2m.at[HALF + k], s_rel.at[HALF + k], q_two.at[MATS + HALF + k], left).start()

    e2[...] = cp[xc]

    @pl.loop(1, XC)
    def _(k):
        q = lax.rem(xc + k, XC)
        arrived(d1.at[q], q_d1.at[q])
        e2[...] += d1[q]

    @pl.loop(1, Y)
    def _(k):
        t = lax.rem(y + k, Y)
        copy(e2.at[t], d2.at[y], s_d2.at[t], q_d2.at[y], (zl * Y + t, inner)).start()

    @pl.loop(0, HALF)
    def _(k):
        arrived(r2m.at[k], q_two.at[HALF + k])
        arrived(r2p.at[k], q_two.at[MATS + k])
        ssum[k] = wp[y, k] + r2p[k] + r2m[k]
        copy(ssum.at[k, 1 - zl], rz.at[k], s_z.at[k], q_z.at[k], pair).start()
        h = HALF + k
        arrived(r2p.at[h], q_two.at[k])
        arrived(r2m.at[h], q_two.at[MATS + h])
        ssum[h] = wp[y, h] + r2p[h] + r2m[h]
        copy(ssum.at[h, 1 - zl], rz.at[h], s_z.at[h], q_z.at[h], pair).start()

    f2[...] = e2[y]

    @pl.loop(1, Y)
    def _(k):
        t = lax.rem(y + k, Y)
        arrived(d2.at[t], q_d2.at[t])
        f2[...] += d2[t]

    copy(f2.at[1 - zl], d3.at[ZHI], s_dz.at[0], q_dz.at[0], pair).start()

    @pl.loop(1, OWNERS)
    def _(k):
        i = lax.rem(inner + k, OWNERS)
        arrived(brec.at[i], q_b.at[i])

    def gather(k, half):
        m = half * HALF + k
        arrived(rz.at[m], q_z.at[m])
        mean = (ssum[m, zl] + rz[m]) * (1.0 / GROUPS)
        avg[m] = mean
        out[y, m, zl] = AVERAGE_PART * mean + brec[list_ref[m]]
        mine = out.at[y, m, zl]
        copy(mine, mine, s_own.at[0, m], q_out.at[y, m, zl], pair).start()
        copy(mine, mine, s_own.at[1, m], q_out.at[y, m, zl], right).start()
        copy(mine, mine, s_own.at[2, m], q_out.at[y, m, zl], left).start()

    @pl.loop(0, HALF)
    def _(k):
        gather(k, 0)
        gather(k, 1)

    @pl.loop(0, OWNERS)
    def _(k):
        i = lax.rem(inner + k, OWNERS)
        picked = jnp.int32(0)
        for m in range(MATS):
            picked = picked + jnp.where(list_ref[m] == i, jnp.int32(m), jnp.int32(0))
        asend[i] = avg[jnp.minimum(picked, MATS - 1)]

    arec[inner] = asend[inner]

    @pl.loop(1, OWNERS)
    def _(k):
        i = lax.rem(inner + k, OWNERS)
        copy(asend.at[i], arec.at[inner], s_a.at[i], q_a.at[inner], (rep, i)).start()

    arrived(d3.at[ZHI], q_dz.at[0])
    g2[...] = f2[zl] + d3[ZHI]

    @pl.loop(1, ZHI)
    def _(k):
        t = lax.rem(zh + k, ZHI)
        copy(g2, d3.at[zh], s_d3.at[t], q_d3.at[zh], (rep, t * XC + xc)).start()

    def forward(m):
        other = out.at[y, m, 1 - zl]
        arrived(other, q_out.at[y, m, 1 - zl])
        copy(other, other, s_fwd.at[0, m], q_out.at[y, m, 1 - zl], right).start()
        copy(other, other, s_fwd.at[1, m], q_out.at[y, m, 1 - zl], left).start()

    @pl.loop(0, HALF)
    def _(k):
        forward(k)
        forward(HALF + k)

    d4[xc] = g2[...]

    @pl.loop(1, ZHI)
    def _(k):
        t = lax.rem(zh + k, ZHI)
        arrived(d3.at[t], q_d3.at[t])
        d4[xc] += d3[t]

    @pl.loop(1, XC)
    def _(k):
        q = lax.rem(xc + k, XC)
        copy(d4.at[xc], d4.at[xc], s_d4.at[q], q_d4.at[xc], (rep, zh * XC + q)).start()

    def relay(k, z):
        a = out.at[down, k, z]
        arrived(a, q_out.at[down, k, z])
        copy(a, a, s_far.at[0, k, z], q_out.at[down, k, z], right).start()
        b = out.at[up, HALF + k, z]
        arrived(b, q_out.at[up, HALF + k, z])
        copy(b, b, s_far.at[1, k, z], q_out.at[up, HALF + k, z], left).start()

    @pl.loop(0, HALF)
    def _(k):
        relay(k, zl)

    @pl.loop(0, HALF)
    def _(k):
        relay(k, 1 - zl)

    @pl.loop(0, HALF)
    def _(k):
        for z in range(ZLO):
            arrived(out.at[down, HALF + k, z], q_out.at[down, HALF + k, z])
            arrived(out.at[up, k, z], q_out.at[up, k, z])
            arrived(out.at[far, k, z], q_out.at[far, k, z])
            arrived(out.at[far, HALF + k, z], q_out.at[far, HALF + k, z])

    @pl.loop(1, XC)
    def _(k):
        q = lax.rem(xc + k, XC)
        arrived(d4.at[q], q_d4.at[q])

    coef[...] = d4[...]

    @pl.loop(1, OWNERS)
    def _(k):
        i = lax.rem(inner + k, OWNERS)
        arrived(arec.at[i], q_a.at[i])

    @pl.loop(0, HALF)
    def _(k):
        left_it(r1p.at[k], s_one.at[k])
        left_it(r1p.at[k], s_one.at[HALF + k])
        left_it(r1p.at[k], s_two.at[k])
        left_it(r1p.at[k], s_two.at[HALF + k])
        left_it(r1p.at[k], s_rel.at[k])
        left_it(r1p.at[k], s_rel.at[HALF + k])
        for h in range(2):
            left_it(rz.at[k], s_z.at[h * HALF + k])
            for n in range(3):
                left_it(rz.at[k], s_own.at[n, h * HALF + k])
            for n in range(2):
                left_it(rz.at[k], s_fwd.at[n, h * HALF + k])
                left_it(rz.at[k], s_far.at[n, k, h])

    @pl.loop(1, OWNERS)
    def _(k):
        i = lax.rem(inner + k, OWNERS)
        left_it(bp.at[i], s_b.at[i])
        left_it(asend.at[i], s_a.at[i])

    @pl.loop(1, XC)
    def _(k):
        q = lax.rem(xc + k, XC)
        left_it(cp.at[q], s_d1.at[q])
        left_it(g2, s_d4.at[q])

    @pl.loop(1, Y)
    def _(k):
        left_it(e2.at[0], s_d2.at[lax.rem(y + k, Y)])
        left_it(g2, s_d3.at[lax.rem(zh + k, ZHI)])

    left_it(g2, s_dz.at[0])


def unpack_kernel(list_ref, p_ref, a_ref, g_ref, m_ref, c_ref, cm_ref, bt_ref, gd_ref,
                  w_ref, mo_ref, nd_ref, cn_ref):
    p = p_ref[:, 0].transpose(1, 0, 2, 3)
    cols = jnp.stack([p[..., SLAB * g : SLAB * (g + 1)] for g in range(FOLD)], axis=2)
    w_ref[0] = cols.reshape(D, SLAB).T

    @pl.when(pl.program_id(0) == 0)
    def _():
        inner = lax.axis_index("inner")
        owns = jnp.int32(0)
        for m in range(MATS):
            owns = owns + jnp.where(list_ref[m] == inner, jnp.int32(1), jnp.int32(0))
        for g in range(FOLD):
            s = slice(SUB * g, SUB * (g + 1))
            mean = jnp.concatenate(
                [a_ref[i][:, SLAB * g : SLAB * (g + 1)] for i in range(OWNERS)], axis=-1
            )
            moment = outer_momentum * m_ref[s] + (g_ref[s] - mean)
            mo_ref[s] = jnp.where(owns > 0, moment, 0.0)

    @pl.when(pl.program_id(0) == 1)
    def _():
        step = c_ref[...].reshape(RANK, LANES)[:, :WIDTH]
        new = outer_momentum * cm_ref[...] + step
        cn_ref[...] = new
        change = lax.dot_general(
            bt_ref[...], step + outer_momentum * new, (((0,), (0,)), ((), ())),
            precision=HIGHEST, preferred_element_type=F32,
        )
        nd_ref[...] = gd_ref[...] - outer_rate * change


def shape(*s):
    return jax.ShapeDtypeStruct(s, F32)


def whole(*s):
    return pl.BlockSpec(s, lambda m: (0,) * len(s))


def on_device(weights, current, moment, owner_list, local_down, global_down, basis, coef_momentum):
    block = (SUB, LANES)
    low = (RANK // XC, LANES)
    g, mo, bt = current[0].T, moment[0].T, basis.T
    vmem = pl.BlockSpec(memory_space=pltpu.VMEM)
    smem = pl.BlockSpec(memory_space=pltpu.SMEM)
    wp, bp, cp = pl.pallas_call(
        pack_kernel,
        grid=(MATS,),
        in_specs=[
            pl.BlockSpec((1, SLAB, D), lambda m: (m, 0, 0)),
            whole(WIDTH, D), whole(WIDTH, D), whole(RANK, WIDTH), whole(WIDTH, D), whole(WIDTH, WIDTH),
        ],
        out_specs=[
            pl.BlockSpec((Y, 1, ZLO) + block, lambda m: (0, m, 0, 0, 0)),
            whole(OWNERS, *block),
            whole(XC, Y, ZLO, *low),
        ],
        out_shape=[shape(Y, MATS, ZLO, *block), shape(OWNERS, *block), shape(XC, Y, ZLO, *low)],
    )(weights[0], g, mo, bt, local_down[0], global_down)

    def buf(*s):
        return pltpu.VMEM(s, F32)

    dma = pltpu.SemaphoreType.DMA
    out, arec, coef = pl.pallas_call(
        comm_kernel,
        in_specs=[smem, vmem, vmem, vmem],
        out_specs=[vmem, vmem, vmem],
        out_shape=[shape(Y, MATS, ZLO, *block), shape(OWNERS, *block), shape(XC, *low)],
        scratch_shapes=[
            buf(HALF, ZLO, *block), buf(HALF, ZLO, *block), buf(MATS, ZLO, *block), buf(MATS, ZLO, *block),
            buf(HALF, ZLO, *block), buf(HALF, ZLO, *block), buf(MATS, *block), buf(MATS, ZLO, *block),
            buf(MATS, *block), buf(OWNERS, *block), buf(OWNERS, *block),
            buf(XC, Y, ZLO, *low), buf(Y, ZLO, *low), buf(ZHI + 1, *low), buf(XC, *low),
            buf(Y, ZLO, *low), buf(ZLO, *low), buf(*low),
            dma((MATS,)), dma((MATS,)), dma((MATS,)), dma((MATS,)), dma((3, MATS)), dma((2, MATS)),
            dma((2, HALF, ZLO)), dma((OWNERS,)), dma((OWNERS,)), dma((XC,)), dma((Y,)), dma((1,)),
            dma((ZHI,)), dma((XC,)),
            dma((MATS,)), dma((2 * MATS,)), dma((MATS,)), dma((Y, MATS, ZLO)), dma((OWNERS,)), dma((OWNERS,)),
            dma((XC,)), dma((Y,)), dma((1,)), dma((ZHI,)), dma((XC,)),
        ],
        compiler_params=pltpu.CompilerParams(has_side_effects=True, vmem_limit_bytes=60 * 2**20),
    )(owner_list, wp, bp, cp)

    new, momentum, new_down, coef_new = pl.pallas_call(
        unpack_kernel,
        grid=(MATS,),
        in_specs=[
            smem,
            pl.BlockSpec((Y, 1, ZLO) + block, lambda m: (0, m, 0, 0, 0)),
            whole(OWNERS, *block), whole(WIDTH, D), whole(WIDTH, D), whole(XC, *low), whole(RANK, WIDTH),
            whole(RANK, WIDTH), whole(WIDTH, WIDTH),
        ],
        out_specs=[
            pl.BlockSpec((1, SLAB, D), lambda m: (m, 0, 0)),
            whole(WIDTH, D), whole(WIDTH, WIDTH), whole(RANK, WIDTH),
        ],
        out_shape=[shape(MATS, SLAB, D), shape(WIDTH, D), shape(WIDTH, WIDTH), shape(RANK, WIDTH)],
    )(owner_list, out, arec, g, mo, coef, coef_momentum, bt, global_down)
    return new, momentum.T[None], new_down, coef_new


def solution(mesh):
    in_specs = (
        P("rep", None, "inner", None),
        P("inner", None, "rep"),
        P("inner", None, "rep"),
        P(),
        P("rep", "inner", None),
        P("inner", "rep"),
        P("inner", None),
        P(None, "rep"),
    )
    out_specs = (P(None, "inner", None), P("inner", None, "rep"), P("inner", "rep"), P(None, "rep"))
    return jax.shard_map(
        on_device, mesh=mesh, in_specs=in_specs, out_specs=out_specs, check_vma=False
    )
```

time: 589 us -> 159 us (0.27)
  waiting for transfers between devices: 487 us -> 0 us
  Pallas kernels: 0 us -> 152 us
  local copies, waits for them, and re-layouts: 41 us -> 4.55 us
  starting transfers between devices: 23.9 us -> 0 us
  between operations: 16.3 us -> 0.64 us
  other arithmetic: 15 us -> 0 us
    psum x1 -> x0, waiting for transfers between devices: 311 us -> none  [on_device(): total = lax.psum(placed - down_local / groups, ('rep', 'inner'))]
    pallas_call x0 -> x3, Pallas kernels: none -> 152 us  [the longest x1 123 us: on_device(): pl.pallas_call(comm_kernel, in_specs=[smem, vmem, vmem, vmem], out_specs=...]
    unnamed x4 -> x0, waiting for transfers between devices: 118 us -> none
    all_to_all x2 -> x0, waiting for transfers between devices: 58.1 us -> none  [the longest x1 30.9 us: on_device(): lax.all_to_all(theta.reshape(owners, slab, width), 'inner', split_axis=0,...]
    all_to_all x2 -> x0, starting transfers between devices: 23.8 us -> none  [the longest x1 14.4 us: on_device(): lax.all_to_all(theta.reshape(owners, slab, width), 'inner', split_axis=0,...]
    unnamed x24 -> x1, local copies, waits for them, and re-layouts: 25.8 us -> 4.55 us
    mul x2 -> x0, other arithmetic: 7.99 us -> none  [the longest x1 5.07 us: on_device(): momentum_out = (moment_new * is_owner)[None]]
    gather x3 -> x0, local copies, waits for them, and re-layouts: 6.43 us -> none  [the longest x2 4.54 us: on_device(): updated = returned[owner_list]]
  transfers between devices with their start and end apart: 5 -> 0, of which waited for: 4 -> 0; matrix products, arithmetic and copies ran while one was open for 4% -> 0% of each run, Pallas kernels for 0% -> 0%
where the time goes in v1:
time: 159 us; the launch traced here: 157 us
  Pallas kernels  152 us (96%)
  local copies, waits for them, and re-layouts  4.55 us (3%)
    pallas_call x1, Pallas kernels, on_device(): pl.pallas_call(comm_kernel, in_specs=[smem, vmem, vmem, vmem], out_specs=...  123 us
    pallas_call x1, Pallas kernels, on_device(): pl.pallas_call(pack_kernel, grid=(MATS,), in_specs=[pl.BlockSpec((1, SLAB...  15.1 us
    pallas_call x1, Pallas kernels, on_device(): pl.pallas_call(unpack_kernel, grid=(MATS,), in_specs=[smem, pl.BlockSpec(...  14.4 us
    unnamed x1, local copies, waits for them, and re-layouts  4.55 us

profile of v1, /device:TPU:1, one launch (start us, length us, event | category | flops | bytes accessed | tf_op | source)
XLA Modules:
  0.0 157.4 jit_solution(6754965021561569504)
XLA Ops:
  0.6 4.5 %copy.14 = f32[1,12,50,1600]{3,2,0,1:T(8,128)} copy(f32[1,12,50,1600]{3,0,2,1:T(1,128)} %param.8) | data formatting | bytes 7680000
  5.2 15.1 %shard_map.111 = (f32[4,12,2,40,256]{4,3,2,1,0:T(8,128)}, f32[32,40,256]{2,1,0:T(8,128)}, f32[8,4,2,8,256]{4,3,2,1,0:T(8,128)}) custom-call(f32[12,50,1600]{2,1,0:T(8,128)} %bitcast.14, f32[200,1600]{1,0:T(8,128)} %bitcast.15, f32[200,1600]{1,0:T(8,128)} %bitcast.17, f32[64,200]{1,0:T(8,128)} %bitcast.20, f32[200,1600]{1,0:T(8,128)} %bitcast.19, ...), custom_call_target="tpu_custom_call" | custom-call | tf_op jit(solution)/shard_map/pallas_call | solution.py:339
  20.2 122.8 %shard_map.112 = (f32[4,12,2,40,256]{4,3,2,1,0:T(8,128)}, f32[32,40,256]{2,1,0:T(8,128)}, f32[8,8,256]{2,1,0:T(8,128)}) custom-call(s32[12]{0:T(128)} %list_ref.3, f32[4,12,2,40,256]{4,3,2,1,0:T(8,128)} %get-tuple-element.14.wp, f32[32,40,256]{2,1,0:T(8,128)} %get-tuple-element.15.bp, f32[8,4,2,8,256]{4,3,2,1,0:T(8,128)} %get-tuple-element.16.cp), custom_call_target="tpu_custom_call" | custom-call | tf_op jit(solution)/shard_map/pallas_call | solution.py:358
  143.0 14.4 %shard_map.113 = (f32[12,50,1600]{2,1,0:T(8,128)}, f32[200,1600]{1,0:T(8,128)}, f32[200,200]{1,0:T(8,128)}, f32[64,200]{1,0:T(8,128)}) custom-call(s32[12]{0:T(128)} %list_ref.3, f32[4,12,2,40,256]{4,3,2,1,0:T(8,128)} %get-tuple-element.17.p_ref, f32[32,40,256]{2,1,0:T(8,128)} %get-tuple-element.18.a_ref, f32[200,1600]{1,0:T(8,128)} %bitcast.16, ...), custom_call_target="tpu_custom_call" | custom-call | tf_op jit(solution)/shard_map/pallas_call | solution.py:378

commit v2 on v1

--- a/solution.py
+++ b/solution.py
@@ -35,32 +35,10 @@
     return jnp.concatenate(list(parts) + [pad], axis=-1)
 
 
-def pack_kernel(w_ref, g_ref, m_ref, bt_ref, ld_ref, gd_ref, wp_ref, bp_ref, cp_ref):
-    cols = w_ref[0].T.reshape(ZLO, Y, FOLD, SUB, SLAB)
-    wp_ref[:, 0] = fold_lanes([cols[:, :, g] for g in range(FOLD)]).transpose(1, 0, 2, 3)
-
-    @pl.when(pl.program_id(0) == 0)
-    def _():
-        b = (CURRENT_PART * g_ref[...] + MOMENT_PART * m_ref[...]).reshape(FOLD, SUB, D)
-        for i in range(OWNERS):
-            bp_ref[i] = fold_lanes([b[g][:, SLAB * i : SLAB * (i + 1)] for g in range(FOLD)])
-
-    @pl.when(pl.program_id(0) == 1)
-    def _():
-        rep = lax.axis_index("rep")
-        local = jnp.dot(bt_ref[...], ld_ref[...], precision=HIGHEST, preferred_element_type=F32)
-        mine = jnp.dot(bt_ref[...], gd_ref[...], precision=HIGHEST, preferred_element_type=F32)
-        pad = jnp.zeros((RANK, LANES - WIDTH), F32)
-        for r in range(GROUPS):
-            part = local[:, WIDTH * r : WIDTH * (r + 1)] * (-1.0 / GROUPS)
-            part = part + jnp.where(rep == r, mine, 0.0)
-            cp_ref[:, r % Y, r // Y] = jnp.concatenate([part, pad], axis=-1).reshape(
-                XC, RANK // XC, LANES
-            )
-
-
 def comm_kernel(
-    list_ref, wp, bp, cp, out, arec, coef,
+    list_ref, w_hbm, g_hbm, m_hbm, ld_hbm, gd_ref, bt_ref, cm_ref,
+    new_hbm, mo_ref, nd_ref, cn_ref,
+    w_in, g_in, m_in, ld_in, cols, new, wp, bp, cp, out, arec, h_in, h_out,
     r1p, r1m, r2p, r2m, sp, sm, rz, ssum, avg, brec, asend,
     d1, d2, d3, d4, e2, f2, g2,
     s_one, s_two, s_rel, s_z, s_own, s_fwd, s_far, s_b, s_a, s_d1, s_d2, s_dz, s_d3, s_d4,
@@ -84,27 +62,81 @@
         copy(src, src, send, q_one.at[0], right).wait_send()
 
 
-    @pl.loop(0, HALF)
-    def _(k):
+    def fetch(m):
+        return pltpu.make_async_copy(w_hbm.at[m, :, 0], w_in.at[m], h_in.at[m])
+
+    @pl.loop(0, HALF)
+    def _(k):
+        fetch(k).start()
+        fetch(HALF + k).start()
+
+    rest = [
+        pltpu.make_async_copy(g_hbm, g_in, h_in.at[MATS]),
+        pltpu.make_async_copy(m_hbm, m_in, h_in.at[MATS + 1]),
+        pltpu.make_async_copy(ld_hbm, ld_in, h_in.at[MATS + 2]),
+    ]
+    for c in rest:
+        c.start()
+
+    barrier = pltpu.get_barrier_semaphore()
+
+    @pl.loop(1, OWNERS)
+    def _(k):
+        pl.semaphore_signal(
+            barrier, inc=1, device_id=(rep, lax.rem(inner + k, OWNERS)), device_id_type=MESH
+        )
+
+    for to in (right, left, (zl * Y + far, inner), pair):
+        pl.semaphore_signal(barrier, inc=1, device_id=to, device_id_type=MESH)
+
+    def pack(m):
+        fetch(m).wait()
+        cols_m = w_in[m].T.reshape(ZLO, Y, FOLD, SUB, SLAB)
+        wp[:, m] = fold_lanes([cols_m[:, :, g] for g in range(FOLD)]).transpose(1, 0, 2, 3)
+
+    def first(k):
         copy(wp.at[far, k], r1p.at[k], s_one.at[k], q_one.at[k], right).start()
         copy(wp.at[far, HALF + k], r1m.at[k], s_one.at[HALF + k], q_one.at[HALF + k], left).start()
+        copy(wp.at[up, HALF + k], r2p.at[HALF + k], s_two.at[k], q_two.at[k], right).start()
+        copy(wp.at[down, k], r2m.at[k], s_two.at[HALF + k], q_two.at[HALF + k], left).start()
+
+    pack(0)
+    pack(HALF)
+    pl.semaphore_wait(barrier, OWNERS + 3)
+    first(0)
+
+    rest[0].wait()
+    rest[1].wait()
+    term = (CURRENT_PART * g_in[...] + MOMENT_PART * m_in[...]).reshape(FOLD, SUB, D)
+    for i in range(OWNERS):
+        bp[i] = fold_lanes([term[g][:, SLAB * i : SLAB * (i + 1)] for g in range(FOLD)])
+
+    @pl.loop(1, OWNERS)
+    def _(k):
+        i = lax.rem(inner + k, OWNERS)
+        copy(bp.at[i], brec.at[inner], s_b.at[i], q_b.at[inner], (rep, i)).start()
+
+    brec[inner] = bp[inner]
+
+    @pl.loop(1, HALF)
+    def _(k):
+        pack(k)
+        pack(HALF + k)
+        first(k)
+
+    rest[2].wait()
+    local = jnp.dot(bt_ref[...], ld_in[...], precision=HIGHEST, preferred_element_type=F32)
+    own = jnp.dot(bt_ref[...], gd_ref[...], precision=HIGHEST, preferred_element_type=F32)
+    pad = jnp.zeros((RANK, LANES - WIDTH), F32)
+    for r in range(GROUPS):
+        part = local[:, WIDTH * r : WIDTH * (r + 1)] * (-1.0 / GROUPS)
+        part = part + jnp.where(rep == r, own, 0.0)
+        cp[:, r % Y, r // Y] = jnp.concatenate([part, pad], axis=-1).reshape(XC, RANK // XC, LANES)
 
     @pl.loop(1, XC)
     def _(k):
         q = lax.rem(xc + k, XC)
         copy(cp.at[q], d1.at[xc], s_d1.at[q], q_d1.at[xc], (rep, zh * XC + q)).start()
-
-    @pl.loop(0, HALF)
-    def _(k):
-        copy(wp.at[up, HALF + k], r2p.at[HALF + k], s_two.at[k], q_two.at[k], right).start()
-        copy(wp.at[down, k], r2m.at[k], s_two.at[HALF + k], q_two.at[HALF + k], left).start()
-
-    @pl.loop(1, OWNERS)
-    def _(k):
-        i = lax.rem(inner + k, OWNERS)
-        copy(bp.at[i], brec.at[inner], s_b.at[i], q_b.at[inner], (rep, i)).start()
-
-    brec[inner] = bp[inner]
 
     @pl.loop(0, HALF)
     def _(k):
@@ -166,6 +198,13 @@
         copy(mine, mine, s_own.at[1, m], q_out.at[y, m, zl], right).start()
         copy(mine, mine, s_own.at[2, m], q_out.at[y, m, zl], left).start()
 
+    def place(t, m, z):
+        p = out[t, m, z]
+        first_col = pl.multiple_of(WIDTH * (z * Y + t), 8)
+        cols[m, pl.ds(first_col, WIDTH), :] = jnp.concatenate(
+            [p[:, SLAB * g : SLAB * (g + 1)] for g in range(FOLD)], axis=0
+        )
+
     @pl.loop(0, HALF)
     def _(k):
         gather(k, 0)
@@ -225,34 +264,70 @@
         b = out.at[up, HALF + k, z]
         arrived(b, q_out.at[up, HALF + k, z])
         copy(b, b, s_far.at[1, k, z], q_out.at[up, HALF + k, z], left).start()
+        place(down, k, z)
+        place(up, HALF + k, z)
 
     @pl.loop(0, HALF)
     def _(k):
         relay(k, zl)
+        place(y, k, zl)
+        place(y, HALF + k, zl)
 
     @pl.loop(0, HALF)
     def _(k):
         relay(k, 1 - zl)
+        place(y, k, 1 - zl)
+        place(y, HALF + k, 1 - zl)
+
+    @pl.loop(1, XC)
+    def _(k):
+        q = lax.rem(xc + k, XC)
+        arrived(d4.at[q], q_d4.at[q])
+
+    step = d4[...].reshape(RANK, LANES)[:, :WIDTH]
+    coef = outer_momentum * cm_ref[...] + step
+    cn_ref[...] = coef
+    change = lax.dot_general(
+        bt_ref[...], step + outer_momentum * coef, (((0,), (0,)), ((), ())),
+        precision=HIGHEST, preferred_element_type=F32,
+    )
+    nd_ref[...] = gd_ref[...] - outer_rate * change
 
     @pl.loop(0, HALF)
     def _(k):
         for z in range(ZLO):
             arrived(out.at[down, HALF + k, z], q_out.at[down, HALF + k, z])
+            place(down, HALF + k, z)
             arrived(out.at[up, k, z], q_out.at[up, k, z])
-            arrived(out.at[far, k, z], q_out.at[far, k, z])
-            arrived(out.at[far, HALF + k, z], q_out.at[far, HALF + k, z])
-
-    @pl.loop(1, XC)
-    def _(k):
-        q = lax.rem(xc + k, XC)
-        arrived(d4.at[q], q_d4.at[q])
-
-    coef[...] = d4[...]
+            place(up, k, z)
+
+    def finish(m):
+        for z in range(ZLO):
+            arrived(out.at[far, m, z], q_out.at[far, m, z])
+            place(far, m, z)
+        new[m] = cols[m].T
+        pltpu.make_async_copy(new.at[m], new_hbm.at[m], h_out.at[m]).start()
+
+    @pl.loop(0, HALF)
+    def _(k):
+        finish(k)
+        finish(HALF + k)
 
     @pl.loop(1, OWNERS)
     def _(k):
         i = lax.rem(inner + k, OWNERS)
         arrived(arec.at[i], q_a.at[i])
+
+    owns = jnp.int32(0)
+    for m in range(MATS):
+        owns = owns + jnp.where(list_ref[m] == inner, jnp.int32(1), jnp.int32(0))
+    for g in range(FOLD):
+        s = slice(SUB * g, SUB * (g + 1))
+        mean = jnp.concatenate(
+            [arec[i][:, SLAB * g : SLAB * (g + 1)] for i in range(OWNERS)], axis=-1
+        )
+        moment = outer_momentum * m_in[s] + (g_in[s] - mean)
+        mo_ref[s] = jnp.where(owns > 0, moment, 0.0)
 
     @pl.loop(0, HALF)
     def _(k):
@@ -289,78 +364,35 @@
 
     left_it(g2, s_dz.at[0])
 
-
-def unpack_kernel(list_ref, p_ref, a_ref, g_ref, m_ref, c_ref, cm_ref, bt_ref, gd_ref,
-                  w_ref, mo_ref, nd_ref, cn_ref):
-    p = p_ref[:, 0].transpose(1, 0, 2, 3)
-    cols = jnp.stack([p[..., SLAB * g : SLAB * (g + 1)] for g in range(FOLD)], axis=2)
-    w_ref[0] = cols.reshape(D, SLAB).T
-
-    @pl.when(pl.program_id(0) == 0)
-    def _():
-        inner = lax.axis_index("inner")
-        owns = jnp.int32(0)
-        for m in range(MATS):
-            owns = owns + jnp.where(list_ref[m] == inner, jnp.int32(1), jnp.int32(0))
-        for g in range(FOLD):
-            s = slice(SUB * g, SUB * (g + 1))
-            mean = jnp.concatenate(
-                [a_ref[i][:, SLAB * g : SLAB * (g + 1)] for i in range(OWNERS)], axis=-1
-            )
-            moment = outer_momentum * m_ref[s] + (g_ref[s] - mean)
-            mo_ref[s] = jnp.where(owns > 0, moment, 0.0)
-
-    @pl.when(pl.program_id(0) == 1)
-    def _():
-        step = c_ref[...].reshape(RANK, LANES)[:, :WIDTH]
-        new = outer_momentum * cm_ref[...] + step
-        cn_ref[...] = new
-        change = lax.dot_general(
-            bt_ref[...], step + outer_momentum * new, (((0,), (0,)), ((), ())),
-            precision=HIGHEST, preferred_element_type=F32,
-        )
-        nd_ref[...] = gd_ref[...] - outer_rate * change
+    @pl.loop(0, MATS)
+    def _(m):
+        pltpu.make_async_copy(new.at[m], new_hbm.at[m], h_out.at[m]).wait()
 
 
 def shape(*s):
     return jax.ShapeDtypeStruct(s, F32)
-
-
-def whole(*s):
-    return pl.BlockSpec(s, lambda m: (0,) * len(s))
 
 
 def on_device(weights, current, moment, owner_list, local_down, global_down, basis, coef_momentum):
     block = (SUB, LANES)
     low = (RANK // XC, LANES)
-    g, mo, bt = current[0].T, moment[0].T, basis.T
     vmem = pl.BlockSpec(memory_space=pltpu.VMEM)
     smem = pl.BlockSpec(memory_space=pltpu.SMEM)
-    wp, bp, cp = pl.pallas_call(
-        pack_kernel,
-        grid=(MATS,),
-        in_specs=[
-            pl.BlockSpec((1, SLAB, D), lambda m: (m, 0, 0)),
-            whole(WIDTH, D), whole(WIDTH, D), whole(RANK, WIDTH), whole(WIDTH, D), whole(WIDTH, WIDTH),
-        ],
-        out_specs=[
-            pl.BlockSpec((Y, 1, ZLO) + block, lambda m: (0, m, 0, 0, 0)),
-            whole(OWNERS, *block),
-            whole(XC, Y, ZLO, *low),
-        ],
-        out_shape=[shape(Y, MATS, ZLO, *block), shape(OWNERS, *block), shape(XC, Y, ZLO, *low)],
-    )(weights[0], g, mo, bt, local_down[0], global_down)
+    hbm = pl.BlockSpec(memory_space=pl.ANY)
 
     def buf(*s):
         return pltpu.VMEM(s, F32)
 
     dma = pltpu.SemaphoreType.DMA
-    out, arec, coef = pl.pallas_call(
+    new, momentum, new_down, coef_new = pl.pallas_call(
         comm_kernel,
-        in_specs=[smem, vmem, vmem, vmem],
-        out_specs=[vmem, vmem, vmem],
-        out_shape=[shape(Y, MATS, ZLO, *block), shape(OWNERS, *block), shape(XC, *low)],
+        in_specs=[smem, hbm, hbm, hbm, hbm, vmem, vmem, vmem],
+        out_specs=[hbm, vmem, vmem, vmem],
+        out_shape=[shape(MATS, SLAB, D), shape(WIDTH, D), shape(WIDTH, WIDTH), shape(RANK, WIDTH)],
         scratch_shapes=[
+            buf(MATS, SLAB, D), buf(WIDTH, D), buf(WIDTH, D), buf(WIDTH, D), buf(MATS, D, SLAB), buf(MATS, SLAB, D),
+            buf(Y, MATS, ZLO, *block), buf(OWNERS, *block), buf(XC, Y, ZLO, *low), buf(Y, MATS, ZLO, *block),
+            buf(OWNERS, *block), dma((MATS + 3,)), dma((MATS,)),
             buf(HALF, ZLO, *block), buf(HALF, ZLO, *block), buf(MATS, ZLO, *block), buf(MATS, ZLO, *block),
             buf(HALF, ZLO, *block), buf(HALF, ZLO, *block), buf(MATS, *block), buf(MATS, ZLO, *block),
             buf(MATS, *block), buf(OWNERS, *block), buf(OWNERS, *block),
@@ -372,24 +404,13 @@
             dma((MATS,)), dma((2 * MATS,)), dma((MATS,)), dma((Y, MATS, ZLO)), dma((OWNERS,)), dma((OWNERS,)),
             dma((XC,)), dma((Y,)), dma((1,)), dma((ZHI,)), dma((XC,)),
         ],
-        compiler_params=pltpu.CompilerParams(has_side_effects=True, vmem_limit_bytes=60 * 2**20),
-    )(owner_list, wp, bp, cp)
-
-    new, momentum, new_down, coef_new = pl.pallas_call(
-        unpack_kernel,
-        grid=(MATS,),
-        in_specs=[
-            smem,
-            pl.BlockSpec((Y, 1, ZLO) + block, lambda m: (0, m, 0, 0, 0)),
-            whole(OWNERS, *block), whole(WIDTH, D), whole(WIDTH, D), whole(XC, *low), whole(RANK, WIDTH),
-            whole(RANK, WIDTH), whole(WIDTH, WIDTH),
-        ],
-        out_specs=[
-            pl.BlockSpec((1, SLAB, D), lambda m: (m, 0, 0)),
-            whole(WIDTH, D), whole(WIDTH, WIDTH), whole(RANK, WIDTH),
-        ],
-        out_shape=[shape(MATS, SLAB, D), shape(WIDTH, D), shape(WIDTH, WIDTH), shape(RANK, WIDTH)],
-    )(owner_list, out, arec, g, mo, coef, coef_momentum, bt, global_down)
+        compiler_params=pltpu.CompilerParams(
+            collective_id=0, has_side_effects=True, vmem_limit_bytes=60 * 2**20
+        ),
+    )(
+        owner_list, weights.reshape(MATS, SLAB, 1, D), current[0].T, moment[0].T, local_down[0],
+        global_down, basis.T, coef_momentum,
+    )
     return new, momentum.T[None], new_down, coef_new
 
 

time: 159 us -> 125 us (0.79)
  Pallas kernels: 152 us -> 114 us
  local copies, waits for them, and re-layouts: 4.55 us -> 7.2 us
    pallas_call x3 -> x1, Pallas kernels: 152 us -> 114 us  [on_device(): pl.pallas_call(comm_kernel, in_specs=[smem, hbm, hbm, hbm, hbm, vmem, vme...]
    unnamed x1 -> x10, local copies, waits for them, and re-layouts: 4.55 us -> 7.2 us
where the time goes in v2:
time: 125 us; the launch traced here: 122 us
  Pallas kernels  114 us (91%)
  local copies, waits for them, and re-layouts  7.2 us (6%)
    pallas_call x1, Pallas kernels, on_device(): pl.pallas_call(comm_kernel, in_specs=[smem, hbm, hbm, hbm, hbm, vmem, vme...  114 us
    unnamed x10, local copies, waits for them, and re-layouts  7.2 us

profile of v2, /device:TPU:1, one launch (start us, length us, event | category | flops | bytes accessed | tf_op | source)
XLA Modules:
  0.0 122.2 jit_solution(13007099742375475821)
XLA Ops:
  0.6 114.4 %shard_map.111 = (f32[12,50,1600]{2,1,0:T(8,128)}, f32[200,1600]{1,0:T(8,128)}, f32[200,200]{1,0:T(8,128)}, f32[64,200]{1,0:T(8,128)}) custom-call(s32[12]{0:T(128)} %list_ref.1, f32[12,50,1,1600]{3,2,1,0:T(1,128)} %bitcast.12, f32[200,1600]{1,0:T(8,128)} %bitcast.14, f32[200,1600]{1,0:T(8,128)} %bitcast.15, f32[200,1600]{1,0:T(8,128)} %bitcast.16, ...), custom_call_target="tpu_custom_call" | custom-call | tf_op jit(solution)/shard_map/pallas_call | solution.py:387
  115.0 0.0 copy-start
  115.0 4.8 %copy.16 = f32[12,50,1600]{2,1,0:T(8,128)} copy(f32[12,50,1600]{2,1,0:T(8,128)} %get-tuple-element.16) | data formatting | bytes 7680000
  119.8 0.0 copy-done
  119.8 0.0 copy-start.1
  119.8 0.0 copy-start.2
  119.8 1.1 copy.17
  120.9 0.1 copy-done.1
  120.9 0.7 copy.18
  121.6 0.0 copy-done.2
  121.6 0.6 copy.19
Async XLA Ops:
  115.0 4.8 %copy-start = (f32[200,1600]{1,0:T(8,128)S(1)}, f32[200,1600]{1,0:T(8,128)}, u32[]{:S(2)}) copy-start(f32[200,1600]{1,0:T(8,128)} %get-tuple-element.9) | copy-start | bytes 3840004
  119.8 1.1 copy-start.1
  119.8 1.8 %copy-start.2 = (f32[64,200]{1,0:T(8,128)S(1)}, f32[64,200]{1,0:T(8,128)}, u32[]{:S(2)}) copy-start(f32[64,200]{1,0:T(8,128)} %get-tuple-element.19) | copy-start | bytes 153604

commit v3 on v2

--- a/solution.py
+++ b/solution.py
@@ -102,27 +102,49 @@
 
     pack(0)
     pack(HALF)
-    pl.semaphore_wait(barrier, OWNERS + 3)
-    first(0)
-
     rest[0].wait()
     rest[1].wait()
     term = (CURRENT_PART * g_in[...] + MOMENT_PART * m_in[...]).reshape(FOLD, SUB, D)
     for i in range(OWNERS):
         bp[i] = fold_lanes([term[g][:, SLAB * i : SLAB * (i + 1)] for g in range(FOLD)])
 
-    @pl.loop(1, OWNERS)
-    def _(k):
-        i = lax.rem(inner + k, OWNERS)
+    pl.semaphore_wait(barrier, OWNERS + 3)
+    first(0)
+
+    def to_owners(send):
+        @pl.loop(0, XC)
+        def _(k):
+            for dz in (2, 1, 3):
+                send(lax.rem(zh + dz, ZHI) * XC + lax.rem(xc + k, XC))
+
+        @pl.loop(1, XC)
+        def _(k):
+            send(zh * XC + lax.rem(xc + k, XC))
+
+    def send_term(i):
         copy(bp.at[i], brec.at[inner], s_b.at[i], q_b.at[inner], (rep, i)).start()
 
+    to_owners(send_term)
     brec[inner] = bp[inner]
 
-    @pl.loop(1, HALF)
+    def second(k):
+        arrived(r1p.at[k], q_one.at[k])
+        sp[k] = r1p[k] + wp[up, k]
+        copy(sp.at[k], r2p.at[k], s_rel.at[k], q_two.at[MATS + k], right).start()
+        arrived(r1m.at[k], q_one.at[HALF + k])
+        sm[k] = r1m[k] + wp[down, HALF + k]
+        copy(sm.at[k], r2m.at[HALF + k], s_rel.at[HALF + k], q_two.at[MATS + HALF + k], left).start()
+
+    pack(1)
+    pack(HALF + 1)
+    first(1)
+
+    @pl.loop(2, HALF)
     def _(k):
         pack(k)
         pack(HALF + k)
         first(k)
+        second(k - 2)
 
     rest[2].wait()
     local = jnp.dot(bt_ref[...], ld_in[...], precision=HIGHEST, preferred_element_type=F32)
@@ -138,27 +160,9 @@
         q = lax.rem(xc + k, XC)
         copy(cp.at[q], d1.at[xc], s_d1.at[q], q_d1.at[xc], (rep, zh * XC + q)).start()
 
-    @pl.loop(0, HALF)
-    def _(k):
-        arrived(r1p.at[k], q_one.at[k])
-        sp[k] = r1p[k] + wp[up, k]
-        copy(sp.at[k], r2p.at[k], s_rel.at[k], q_two.at[MATS + k], right).start()
-        arrived(r1m.at[k], q_one.at[HALF + k])
-        sm[k] = r1m[k] + wp[down, HALF + k]
-        copy(sm.at[k], r2m.at[HALF + k], s_rel.at[HALF + k], q_two.at[MATS + HALF + k], left).start()
-
-    e2[...] = cp[xc]
-
-    @pl.loop(1, XC)
-    def _(k):
-        q = lax.rem(xc + k, XC)
-        arrived(d1.at[q], q_d1.at[q])
-        e2[...] += d1[q]
-
-    @pl.loop(1, Y)
-    def _(k):
-        t = lax.rem(y + k, Y)
-        copy(e2.at[t], d2.at[y], s_d2.at[t], q_d2.at[y], (zl * Y + t, inner)).start()
+    @pl.loop(HALF - 2, HALF)
+    def _(k):
+        second(k)
 
     @pl.loop(0, HALF)
     def _(k):
@@ -172,15 +176,18 @@
         ssum[h] = wp[y, h] + r2p[h] + r2m[h]
         copy(ssum.at[h, 1 - zl], rz.at[h], s_z.at[h], q_z.at[h], pair).start()
 
-    f2[...] = e2[y]
+    e2[...] = cp[xc]
+
+    @pl.loop(1, XC)
+    def _(k):
+        q = lax.rem(xc + k, XC)
+        arrived(d1.at[q], q_d1.at[q])
+        e2[...] += d1[q]
 
     @pl.loop(1, Y)
     def _(k):
         t = lax.rem(y + k, Y)
-        arrived(d2.at[t], q_d2.at[t])
-        f2[...] += d2[t]
-
-    copy(f2.at[1 - zl], d3.at[ZHI], s_dz.at[0], q_dz.at[0], pair).start()
+        copy(e2.at[t], d2.at[y], s_d2.at[t], q_d2.at[y], (zl * Y + t, inner)).start()
 
     @pl.loop(1, OWNERS)
     def _(k):
@@ -210,28 +217,28 @@
         gather(k, 0)
         gather(k, 1)
 
-    @pl.loop(0, OWNERS)
-    def _(k):
-        i = lax.rem(inner + k, OWNERS)
+    def pick(i):
         picked = jnp.int32(0)
         for m in range(MATS):
             picked = picked + jnp.where(list_ref[m] == i, jnp.int32(m), jnp.int32(0))
-        asend[i] = avg[jnp.minimum(picked, MATS - 1)]
-
-    arec[inner] = asend[inner]
-
-    @pl.loop(1, OWNERS)
-    def _(k):
-        i = lax.rem(inner + k, OWNERS)
+        return avg[jnp.minimum(picked, MATS - 1)]
+
+    def send_average(i):
+        asend[i] = pick(i)
         copy(asend.at[i], arec.at[inner], s_a.at[i], q_a.at[inner], (rep, i)).start()
 
-    arrived(d3.at[ZHI], q_dz.at[0])
-    g2[...] = f2[zl] + d3[ZHI]
-
-    @pl.loop(1, ZHI)
-    def _(k):
-        t = lax.rem(zh + k, ZHI)
-        copy(g2, d3.at[zh], s_d3.at[t], q_d3.at[zh], (rep, t * XC + xc)).start()
+    to_owners(send_average)
+    arec[inner] = pick(inner)
+
+    f2[...] = e2[y]
+
+    @pl.loop(1, Y)
+    def _(k):
+        t = lax.rem(y + k, Y)
+        arrived(d2.at[t], q_d2.at[t])
+        f2[...] += d2[t]
+
+    copy(f2.at[1 - zl], d3.at[ZHI], s_dz.at[0], q_dz.at[0], pair).start()
 
     def forward(m):
         other = out.at[y, m, 1 - zl]
@@ -244,18 +251,13 @@
         forward(k)
         forward(HALF + k)
 
-    d4[xc] = g2[...]
+    arrived(d3.at[ZHI], q_dz.at[0])
+    g2[...] = f2[zl] + d3[ZHI]
 
     @pl.loop(1, ZHI)
     def _(k):
         t = lax.rem(zh + k, ZHI)
-        arrived(d3.at[t], q_d3.at[t])
-        d4[xc] += d3[t]
-
-    @pl.loop(1, XC)
-    def _(k):
-        q = lax.rem(xc + k, XC)
-        copy(d4.at[xc], d4.at[xc], s_d4.at[q], q_d4.at[xc], (rep, zh * XC + q)).start()
+        copy(g2, d3.at[zh], s_d3.at[t], q_d3.at[zh], (rep, t * XC + xc)).start()
 
     def relay(k, z):
         a = out.at[down, k, z]
@@ -272,6 +274,19 @@
         relay(k, zl)
         place(y, k, zl)
         place(y, HALF + k, zl)
+
+    d4[xc] = g2[...]
+
+    @pl.loop(1, ZHI)
+    def _(k):
+        t = lax.rem(zh + k, ZHI)
+        arrived(d3.at[t], q_d3.at[t])
+        d4[xc] += d3[t]
+
+    @pl.loop(1, XC)
+    def _(k):
+        q = lax.rem(xc + k, XC)
+        copy(d4.at[xc], d4.at[xc], s_d4.at[q], q_d4.at[xc], (rep, zh * XC + q)).start()
 
     @pl.loop(0, HALF)
     def _(k):

time: 125 us -> 124 us (level); the launches traced: 122 us -> 124 us
  Pallas kernels: 114 us -> 116 us
    pallas_call x1, Pallas kernels: 114 us -> 116 us  [on_device(): pl.pallas_call(comm_kernel, in_specs=[smem, hbm, hbm, hbm, hbm, vmem, vme...]
where the time goes in v3:
time: 124 us
  Pallas kernels  116 us (94%)
  local copies, waits for them, and re-layouts  7.2 us (6%)
    pallas_call x1, Pallas kernels, on_device(): pl.pallas_call(comm_kernel, in_specs=[smem, hbm, hbm, hbm, hbm, vmem, vme...  116 us
    unnamed x10, local copies, waits for them, and re-layouts  7.2 us

profile of v3, /device:TPU:1, one launch (start us, length us, event | category | flops | bytes accessed | tf_op | source)
XLA Modules:
  0.0 123.5 jit_solution(670050646691882354)
XLA Ops:
  0.6 115.7 %shard_map.111 = (f32[12,50,1600]{2,1,0:T(8,128)}, f32[200,1600]{1,0:T(8,128)}, f32[200,200]{1,0:T(8,128)}, f32[64,200]{1,0:T(8,128)}) custom-call(s32[12]{0:T(128)} %list_ref.1, f32[12,50,1,1600]{3,2,1,0:T(1,128)} %bitcast.12, f32[200,1600]{1,0:T(8,128)} %bitcast.14, f32[200,1600]{1,0:T(8,128)} %bitcast.15, f32[200,1600]{1,0:T(8,128)} %bitcast.16, ...), custom_call_target="tpu_custom_call" | custom-call | tf_op jit(solution)/shard_map/pallas_call | solution.py:402
  116.3 0.0 copy-start
  116.3 4.8 %copy.16 = f32[12,50,1600]{2,1,0:T(8,128)} copy(f32[12,50,1600]{2,1,0:T(8,128)} %get-tuple-element.16) | data formatting | bytes 7680000
  121.1 0.0 copy-done
  121.1 0.0 copy-start.1
  121.1 0.0 copy-start.2
  121.1 1.1 copy.17
  122.2 0.1 copy-done.1
  122.2 0.7 copy.18
  122.9 0.0 copy-done.2
  122.9 0.6 copy.19
Async XLA Ops:
  116.3 4.8 %copy-start = (f32[200,1600]{1,0:T(8,128)S(1)}, f32[200,1600]{1,0:T(8,128)}, u32[]{:S(2)}) copy-start(f32[200,1600]{1,0:T(8,128)} %get-tuple-element.9) | copy-start | bytes 3840004
  121.1 1.1 copy-start.1
  121.1 1.8 %copy-start.2 = (f32[64,200]{1,0:T(8,128)S(1)}, f32[64,200]{1,0:T(8,128)}, u32[]{:S(2)}) copy-start(f32[64,200]{1,0:T(8,128)} %get-tuple-element.19) | copy-start | bytes 153604

commit v4 on v3

--- a/solution.py
+++ b/solution.py
@@ -288,11 +288,35 @@
         q = lax.rem(xc + k, XC)
         copy(d4.at[xc], d4.at[xc], s_d4.at[q], q_d4.at[xc], (rep, zh * XC + q)).start()
 
-    @pl.loop(0, HALF)
-    def _(k):
+    def finish(m):
+        for z in range(ZLO):
+            arrived(out.at[far, m, z], q_out.at[far, m, z])
+            place(far, m, z)
+        new[m] = cols[m].T
+        pltpu.make_async_copy(new.at[m], new_hbm.at[m], h_out.at[m]).start()
+
+    def complete(k):
+        for z in range(ZLO):
+            arrived(out.at[down, HALF + k, z], q_out.at[down, HALF + k, z])
+            place(down, HALF + k, z)
+            arrived(out.at[up, k, z], q_out.at[up, k, z])
+            place(up, k, z)
+        finish(k)
+        finish(HALF + k)
+
+    def last_relay(k):
         relay(k, 1 - zl)
         place(y, k, 1 - zl)
         place(y, HALF + k, 1 - zl)
+
+    @pl.loop(0, 2)
+    def _(k):
+        last_relay(k)
+
+    @pl.loop(2, HALF)
+    def _(k):
+        last_relay(k)
+        complete(k - 2)
 
     @pl.loop(1, XC)
     def _(k):
@@ -308,25 +332,9 @@
     )
     nd_ref[...] = gd_ref[...] - outer_rate * change
 
-    @pl.loop(0, HALF)
-    def _(k):
-        for z in range(ZLO):
-            arrived(out.at[down, HALF + k, z], q_out.at[down, HALF + k, z])
-            place(down, HALF + k, z)
-            arrived(out.at[up, k, z], q_out.at[up, k, z])
-            place(up, k, z)
-
-    def finish(m):
-        for z in range(ZLO):
-            arrived(out.at[far, m, z], q_out.at[far, m, z])
-            place(far, m, z)
-        new[m] = cols[m].T
-        pltpu.make_async_copy(new.at[m], new_hbm.at[m], h_out.at[m]).start()
-
-    @pl.loop(0, HALF)
-    def _(k):
-        finish(k)
-        finish(HALF + k)
+    @pl.loop(HALF - 2, HALF)
+    def _(k):
+        complete(k)
 
     @pl.loop(1, OWNERS)
     def _(k):

time: 124 us -> 124 us (level)
  no operation moved by 1% of the time
where the time goes in v4:
time: 124 us
  Pallas kernels  116 us (94%)
  local copies, waits for them, and re-layouts  7.2 us (6%)
    pallas_call x1, Pallas kernels, on_device(): pl.pallas_call(comm_kernel, in_specs=[smem, hbm, hbm, hbm, hbm, vmem, vme...  116 us
    unnamed x10, local copies, waits for them, and re-layouts  7.2 us

profile of v4, /device:TPU:1, one launch (start us, length us, event | category | flops | bytes accessed | tf_op | source)
XLA Modules:
  0.0 123.7 jit_solution(12331282213155669212)
XLA Ops:
  0.6 115.8 %shard_map.111 = (f32[12,50,1600]{2,1,0:T(8,128)}, f32[200,1600]{1,0:T(8,128)}, f32[200,200]{1,0:T(8,128)}, f32[64,200]{1,0:T(8,128)}) custom-call(s32[12]{0:T(128)} %list_ref.1, f32[12,50,1,1600]{3,2,1,0:T(1,128)} %bitcast.12, f32[200,1600]{1,0:T(8,128)} %bitcast.14, f32[200,1600]{1,0:T(8,128)} %bitcast.15, f32[200,1600]{1,0:T(8,128)} %bitcast.16, ...), custom_call_target="tpu_custom_call" | custom-call | tf_op jit(solution)/shard_map/pallas_call | solution.py:410
  116.5 0.0 copy-start
  116.5 4.8 %copy.16 = f32[12,50,1600]{2,1,0:T(8,128)} copy(f32[12,50,1600]{2,1,0:T(8,128)} %get-tuple-element.16) | data formatting | bytes 7680000
  121.3 0.0 copy-done
  121.3 0.0 copy-start.1
  121.3 0.0 copy-start.2
  121.3 1.1 copy.17
  122.3 0.1 copy-done.1
  122.4 0.7 copy.18
  123.1 0.0 copy-done.2
  123.1 0.6 copy.19
Async XLA Ops:
  116.5 4.8 %copy-start = (f32[200,1600]{1,0:T(8,128)S(1)}, f32[200,1600]{1,0:T(8,128)}, u32[]{:S(2)}) copy-start(f32[200,1600]{1,0:T(8,128)} %get-tuple-element.9) | copy-start | bytes 3840004
  121.3 1.1 copy-start.1
  121.3 1.8 %copy-start.2 = (f32[64,200]{1,0:T(8,128)S(1)}, f32[64,200]{1,0:T(8,128)}, u32[]{:S(2)}) copy-start(f32[64,200]{1,0:T(8,128)} %get-tuple-element.19) | copy-start | bytes 153604
